TPU v7x, 32 devices: a whole 2x2x4 slice. The times are simulated.
32 devices in a mesh: rows: 4 (over x, core), feat: 8 (over z, y).
Axes of the slice: x: 2, y: 2, z: 4, core: 2. Of those that a mesh axis runs over, the one named last changes fastest.
Arguments:
- embeddings: bfloat16 [512, 1024], P(('rows', 'feat')), may hold values from -12 to 12
- freqs: bfloat16 [1024, 65536], P(None, 'feat'), may hold values from -0.1875 to 0.1875
- phases: float32 [65536], P('feat'), may hold values from 0 to 6.2831855
- sketch: bfloat16 [65536, 256], P('feat'), may hold values from -0.0234375 to 0.0234375
Outputs:
- basis: float32 [512, 256], P(('rows', 'feat'))
- coeffs: float32 [256, 65536], P(None, 'feat')
All inputs are finite; a program needn't handle non-finite values.
Results may differ from a plain program's by a relative error of at most 0.0048.
Values may be sent and summed in bfloat16 or wider, within the bound.
A program may use at most 128 MiB of HBM per device.

v0:
```python
import jax
import jax.numpy as jnp
from jax import lax
from jax.sharding import PartitionSpec as P


def per_device(embeddings, freqs, phases, sketch):
    rows_dev = embeddings.shape[0]
    row_count = rows_dev * lax.axis_size("feat") * lax.axis_size("rows")
    mixed = jnp.dot(
        lax.all_gather(embeddings, "feat", axis=0, tiled=True),
        freqs,
        preferred_element_type=jnp.float32,
    )
    features = jnp.cos(mixed + phases).astype(jnp.bfloat16)
    owned_rows = lax.psum_scatter(
        jnp.dot(features, sketch, preferred_element_type=jnp.float32),
        "feat",
        scatter_dimension=0,
        tiled=True,
    )
    local_gram = jnp.dot(owned_rows.T, owned_rows, precision=lax.Precision.HIGHEST)
    gram_matrix = lax.psum(local_gram, ("rows", "feat")) / row_count
    factor = jnp.linalg.cholesky(gram_matrix)
    basis = jax.scipy.linalg.solve_triangular(factor, owned_rows.T, lower=True).T
    block_basis = lax.all_gather(basis.astype(jnp.bfloat16), "feat", axis=0, tiled=True)
    partial_value = lax.dot_general(
        block_basis, features, (((0,), (0,)), ((), ())), preferred_element_type=jnp.float32
    )
    coeffs = lax.psum(partial_value, "rows") / row_count
    return (basis, coeffs)


def solution(mesh):
    placed = (P(("rows", "feat"), None), P(None, "feat"), P("feat"), P("feat", None))
    return jax.shard_map(
        per_device,
        mesh=mesh,
        in_specs=placed,
        out_specs=(P(("rows", "feat"), None), P(None, "feat")),
        check_vma=False,
    )
```

profile of v0, /device:TPU:0, one launch (start us, length us, event | category | flops | bytes accessed | tf_op | source)
XLA Modules:
  0.0 516.5 jit_solution(3243274491165157878)
XLA Ops:
  7.2 0.0 reduce-scatter.2.cloned.1.call-start
  7.2 32.7 %all_gather.6 = bf16[128,1024]{1,0:T(8,128)(2,1)S(1)} all-gather(bf16[16,1024]{1,0:T(8,128)(2,1)} %param.4), channel_id=1, replica_groups=mesh['rows'=4,'feat'=8] {'feat'}, dimensions={0}, use_global_device_ids=true | all-gather | bytes 294912 | tf_op jit(solution)/shard_map/all_gather | solution.py:11
  39.9 0.0 copy-start
  40.0 18.1 %fusion.1 = bf16[128,8192]{1,0:T(8,128)(2,1)S(1)} fusion(bf16[128,1024]{1,0:T(8,128)(2,1)S(1)} %all_gather.6, bf16[1024,8192]{1,0:T(8,128)(2,1)} %param.5, f32[8192]{0:T(1024)} %param.6), kind=kOutput, calls=%fused_computation.4 | convolution fusion | flops 2149580800 | bytes 19169280 | tf_op jit(solution)/shard_map/dot_general | solution.py:10
  58.1 0.0 copy-done
  58.1 1.5 fusion.12
  59.6 0.0 reduce-scatter.2.cloned.1.call-update
  59.6 0.0 all-reduce.4.cloned.1.call-start
  59.6 62.0 %reduce-scatter.2.cloned.1.call-done = f32[16,256]{1,0:T(8,128)} async-done(((f32[128,256]{1,0:T(8,128)}), f32[16,256]{1,0:T(8,128)}) %reduce-scatter.2.cloned.1.call-update) | async-done | bytes 16400 | tf_op jit(solution)/shard_map/reduce_scatter | solution.py:16
  121.6 0.0 copy-start.1
  121.6 1.9 fusion.13
  123.6 0.0 all-reduce.4.cloned.1.call-update
  123.6 0.2 all-reduce.6.cloned.1.call-start
  123.8 128.0 %all-reduce.4.cloned.1.call-done = f32[256,256]{0,1:T(8,128)} async-done(((f32[256,256]{0,1:T(8,128)}), f32[256,256]{0,1:T(8,128)}) %all-reduce.4.cloned.1.call-update) | async-done | bytes 262160 | tf_op jit(solution)/shard_map/psum | solution.py:23
  251.8 1.0 broadcast_multiply_fusion.1
  252.8 0.1 copy.7
  252.9 1.0 fusion.2
  253.9 11.7 %cholesky.50 = f32[128,128]{1,0:T(8,128)S(1)} custom-call(f32[128,128]{1,0:T(8,128)S(1)} %cholesky.118), custom_call_target="Cholesky" | custom-call | tf_op jit(solution)/shard_map/jit(cholesky)/cholesky | solution.py:24
  265.7 9.8 %custom-call.15 = f32[1,128,128]{1,2,0:T(8,128)S(1)} custom-call(f32[1,128,128]{2,1,0:T(8,128)S(1)} %get-tuple-element.25), custom_call_target="InvertDiagBlocksLowerTriangular" | custom-call | tf_op jit(solution)/shard_map/jit(cholesky)/cholesky | solution.py:24
  275.5 0.2 constant_dynamic-update-slice_fusion.1
  275.7 0.3 convolution_subtract_fusion
  276.0 11.7 %cholesky.105 = f32[128,128]{1,0:T(8,128)S(1)} custom-call(f32[128,128]{1,0:T(8,128)S(1)} %convolution_subtract_fusion), custom_call_target="Cholesky" | custom-call | tf_op jit(solution)/shard_map/jit(cholesky)/cholesky | solution.py:24
  287.8 0.7 compare_reduce_fusion
  289.9 0.1 triangular_solve.57
  289.9 4.3 while.1
  290.1 0.6 fusion.28
  290.7 1.4 bitcast_dynamic-update-slice_fusion.2
  292.2 0.6 fusion.28
  292.8 1.4 bitcast_dynamic-update-slice_fusion.2
  294.2 19.7 %custom-call.16 = f32[2,128,128]{1,2,0:T(8,128)S(1)} custom-call(f32[2,128,128]{2,1,0:T(8,128)S(1)} %get-tuple-element.9), custom_call_target="InvertDiagBlocksLowerTriangular" | custom-call | tf_op jit(solution)/shard_map/jit(_solve_triangular)/triangular_solve | solution.py:25
  313.9 0.0 copy-done.1
  313.9 0.2 fusion.5
  314.1 0.2 convolution_subtract_fusion.1
  314.3 0.2 fusion.4
  314.5 0.6 fusion.10
  315.1 30.5 %all_gather.7 = bf16[128,256]{1,0:T(8,128)(2,1)S(1)} all-gather(bf16[16,256]{1,0:T(8,128)(2,1)S(1)} %get-tuple-element.18), channel_id=1, replica_groups=mesh['rows'=4,'feat'=8] {'feat'}, dimensions={0}, use_global_device_ids=true | all-gather | bytes 73728 | tf_op jit(solution)/shard_map/all_gather | solution.py:26
  345.6 4.7 fusion.14
  350.3 0.0 all-reduce.6.cloned.1.call-update
  350.3 152.0 %all-reduce.6.cloned.1.call-done = f32[256,8192]{1,0:T(8,128)} async-done(((f32[256,8192]{1,0:T(8,128)}), f32[256,8192]{1,0:T(8,128)}) %all-reduce.6.cloned.1.call-update) | async-done | bytes 8388624 | tf_op jit(solution)/shard_map/psum | solution.py:30
  502.3 7.7 %broadcast_multiply_fusion = f32[256,8192]{1,0:T(8,128)} fusion(f32[256,8192]{1,0:T(8,128)} %all-reduce.6.cloned.1.call-done), kind=kLoop, calls=%fused_computation.5 | loop fusion | flops 2097152 | bytes 16777216 | tf_op jit(solution)/shard_map/div | solution.py:30
  (9 shorter events, 0.1 us)
Async XLA Ops:
  7.2 114.5 %reduce-scatter.2.cloned.1.call-start = ((), (), s32[]{:S(2)}) async-start(), calls=%async_computation.1 | async-start | bytes 147456 | tf_op jit(solution)/shard_map/reduce_scatter | solution.py:16
  39.9 18.2 %copy-start = (bf16[8192,256]{1,0:T(8,128)(2,1)S(1)}, bf16[8192,256]{1,0:T(8,128)(2,1)}, u32[]{:S(2)}) copy-start(bf16[8192,256]{1,0:T(8,128)(2,1)} %param.7) | copy-start | bytes 12582916
  59.6 192.2 %all-reduce.4.cloned.1.call-start = ((), (), s32[]{:S(2)}) async-start(), calls=%async_computation.2 | async-start | bytes 524288 | tf_op jit(solution)/shard_map/psum | solution.py:23
  121.6 192.3 %copy-start.1 = (f32[16,256]{1,0:T(8,128)S(1)}, f32[16,256]{1,0:T(8,128)}, u32[]{:S(2)}) copy-start(f32[16,256]{1,0:T(8,128)} %reduce-scatter.2.cloned.1.call-done) | copy-start | bytes 49156
  123.6 378.7 %all-reduce.6.cloned.1.call-start = ((), (), s32[]{:S(2)}) async-start(), calls=%async_computation.3 | async-start | bytes 16777216 | tf_op jit(solution)/shard_map/psum | solution.py:30
Sparse Core Ops, SparseCore 0:
  59.7 61.8 reduce-scatter.1
  127.7 124.0 all-reduce.3
  350.4 151.8 all-reduce.5
where the time goes:
time: 517 us
  waiting for transfers between devices  342 us (66%)
  other arithmetic  64 us (12%)
  blocking collectives  63.2 us (12%)
  matrix products  27.2 us (5%)
  between operations  15.2 us (3%)
    psum x1, waiting for transfers between devices, per_device(): coeffs = lax.psum(partial_value, 'rows') / row_count  152 us
    psum x1, waiting for transfers between devices, per_device(): gram_matrix = lax.psum(local_gram, ('rows', 'feat')) / row_count  128 us
    reduce_scatter x1, waiting for transfers between devices, per_device(): lax.psum_scatter(jnp.dot(features, sketch, preferred_element_type=jnp.flo...  62 us
    another operation x6, other arithmetic, per_device(): factor = jnp.linalg.cholesky(gram_matrix)  34 us
    all_gather x1, blocking collectives, per_device(): lax.all_gather(embeddings, 'feat', axis=0, tiled=True)  32.7 us
    all_gather x1, blocking collectives, per_device(): lax.all_gather(basis.astype(jnp.bfloat16), 'feat', axis=0, tiled=True)  30.5 us
    another operation x3, other arithmetic, per_device(): jax.scipy.linalg.solve_triangular(factor, owned_rows.T, lower=True)  19.7 us
    dot_general x1, matrix products, per_device(): jnp.dot(lax.all_gather(embeddings, 'feat', axis=0, tiled=True), freqs, pr...  18.1 us
  transfers between devices with their start and end apart: 3, of which 3 were waited for; matrix products, arithmetic and copies ran while one was open for 0% of the time, Pallas kernels for 0%

commit v1 on v0

--- a/solution.py
+++ b/solution.py
@@ -20,7 +20,7 @@
         tiled=True,
     )
     local_gram = jnp.dot(owned_rows.T, owned_rows, precision=lax.Precision.HIGHEST)
-    gram_matrix = lax.psum(local_gram, ("rows", "feat")) / row_count
+    gram_matrix = lax.psum(lax.psum(local_gram, "feat"), "rows") / row_count
     factor = jnp.linalg.cholesky(gram_matrix)
     basis = jax.scipy.linalg.solve_triangular(factor, owned_rows.T, lower=True).T
     block_basis = lax.all_gather(basis.astype(jnp.bfloat16), "feat", axis=0, tiled=True)

time: 517 us -> 495 us (0.957)
  waiting for transfers between devices: 342 us -> 320 us
    psum x1 -> x2, waiting for transfers between devices: 128 us -> 105 us  [per_device(): gram_matrix = lax.psum(lax.psum(local_gram, 'feat'), 'rows') / row_count]
  transfers between devices with their start and end apart: 3 -> 4, of which waited for: 3 -> 4; matrix products, arithmetic and copies ran while one was open for 0% -> 0% of each run, Pallas kernels for 0% -> 0%
where the time goes in v1:
time: 495 us
  waiting for transfers between devices  320 us (65%)
  other arithmetic  64 us (13%)
  blocking collectives  63.3 us (13%)
  matrix products  27.2 us (5%)
  between operations  15.2 us (3%)
    psum x1, waiting for transfers between devices, per_device(): coeffs = lax.psum(partial_value, 'rows') / row_count  153 us
    psum x2, waiting for transfers between devices, per_device(): gram_matrix = lax.psum(lax.psum(local_gram, 'feat'), 'rows') / row_count  105 us
    reduce_scatter x1, waiting for transfers between devices, per_device(): lax.psum_scatter(jnp.dot(features, sketch, preferred_element_type=jnp.flo...  62 us
    another operation x6, other arithmetic, per_device(): factor = jnp.linalg.cholesky(gram_matrix)  34 us
    all_gather x1, blocking collectives, per_device(): lax.all_gather(embeddings, 'feat', axis=0, tiled=True)  32.7 us
    all_gather x1, blocking collectives, per_device(): lax.all_gather(basis.astype(jnp.bfloat16), 'feat', axis=0, tiled=True)  30.6 us
    another operation x3, other arithmetic, per_device(): jax.scipy.linalg.solve_triangular(factor, owned_rows.T, lower=True)  19.7 us
    dot_general x1, matrix products, per_device(): jnp.dot(lax.all_gather(embeddings, 'feat', axis=0, tiled=True), freqs, pr...  18.1 us
  transfers between devices with their start and end apart: 4, of which 4 were waited for; matrix products, arithmetic and copies ran while one was open for 0% of the time, Pallas kernels for 0%

profile of v1, /device:TPU:0, one launch (start us, length us, event | category | flops | bytes accessed | tf_op | source)
XLA Modules:
  0.0 494.6 jit_solution(12629000864545139548)
XLA Ops:
  7.2 0.0 reduce-scatter.2.cloned.1.call-start
  7.2 32.7 %all_gather.6 = bf16[128,1024]{1,0:T(8,128)(2,1)S(1)} all-gather(bf16[16,1024]{1,0:T(8,128)(2,1)} %param.4), channel_id=1, replica_groups=mesh['rows'=4,'feat'=8] {'feat'}, dimensions={0}, use_global_device_ids=true | all-gather | bytes 294912 | tf_op jit(solution)/shard_map/all_gather | solution.py:11
  39.9 0.0 copy-start
  40.0 18.1 %fusion.1 = bf16[128,8192]{1,0:T(8,128)(2,1)S(1)} fusion(bf16[128,1024]{1,0:T(8,128)(2,1)S(1)} %all_gather.6, bf16[1024,8192]{1,0:T(8,128)(2,1)} %param.5, f32[8192]{0:T(1024)} %param.6), kind=kOutput, calls=%fused_computation.4 | convolution fusion | flops 2149580800 | bytes 19169280 | tf_op jit(solution)/shard_map/dot_general | solution.py:10
  58.1 0.0 copy-done
  58.1 1.5 fusion.12
  59.6 0.0 reduce-scatter.2.cloned.1.call-update
  59.6 0.0 all-reduce.5.cloned.1.call-start
  59.6 62.0 %reduce-scatter.2.cloned.1.call-done = f32[16,256]{1,0:T(8,128)} async-done(((f32[128,256]{1,0:T(8,128)}), f32[16,256]{1,0:T(8,128)}) %reduce-scatter.2.cloned.1.call-update) | async-done | bytes 16400 | tf_op jit(solution)/shard_map/reduce_scatter | solution.py:16
  121.6 0.0 copy-start.1
  121.6 1.9 fusion.13
  123.6 0.0 all-reduce.5.cloned.1.call-update
  123.6 0.0 all-reduce.7.cloned.1.call-start
  123.6 71.5 %all-reduce.5.cloned.1.call-done = f32[256,256]{0,1:T(8,128)} async-done(((f32[256,256]{0,1:T(8,128)}), f32[256,256]{0,1:T(8,128)}) %all-reduce.5.cloned.1.call-update) | async-done | bytes 262160 | tf_op jit(solution)/shard_map/psum | solution.py:23
  195.2 0.0 all-reduce.7.cloned.1.call-update
  195.2 0.2 all-reduce.9.cloned.1.call-start
  195.4 33.5 %all-reduce.7.cloned.1.call-done = f32[256,256]{0,1:T(8,128)} async-done(((f32[256,256]{0,1:T(8,128)}), f32[256,256]{0,1:T(8,128)}) %all-reduce.7.cloned.1.call-update) | async-done | bytes 262160 | tf_op jit(solution)/shard_map/psum | solution.py:23
  228.9 1.0 broadcast_multiply_fusion.1
  229.9 0.1 copy.7
  230.0 1.0 fusion.2
  231.0 11.7 %cholesky.50 = f32[128,128]{1,0:T(8,128)S(1)} custom-call(f32[128,128]{1,0:T(8,128)S(1)} %cholesky.118), custom_call_target="Cholesky" | custom-call | tf_op jit(solution)/shard_map/jit(cholesky)/cholesky | solution.py:24
  242.8 9.8 %custom-call.15 = f32[1,128,128]{1,2,0:T(8,128)S(1)} custom-call(f32[1,128,128]{2,1,0:T(8,128)S(1)} %get-tuple-element.25), custom_call_target="InvertDiagBlocksLowerTriangular" | custom-call | tf_op jit(solution)/shard_map/jit(cholesky)/cholesky | solution.py:24
  252.6 0.2 constant_dynamic-update-slice_fusion.1
  252.8 0.3 convolution_subtract_fusion
  253.1 11.7 %cholesky.105 = f32[128,128]{1,0:T(8,128)S(1)} custom-call(f32[128,128]{1,0:T(8,128)S(1)} %convolution_subtract_fusion), custom_call_target="Cholesky" | custom-call | tf_op jit(solution)/shard_map/jit(cholesky)/cholesky | solution.py:24
  264.8 0.7 compare_reduce_fusion
  266.9 0.1 triangular_solve.57
  267.0 4.3 while.1
  267.2 0.6 fusion.28
  267.8 1.4 bitcast_dynamic-update-slice_fusion.2
  269.3 0.6 fusion.28
  269.9 1.4 bitcast_dynamic-update-slice_fusion.2
  271.3 19.7 %custom-call.16 = f32[2,128,128]{1,2,0:T(8,128)S(1)} custom-call(f32[2,128,128]{2,1,0:T(8,128)S(1)} %get-tuple-element.9), custom_call_target="InvertDiagBlocksLowerTriangular" | custom-call | tf_op jit(solution)/shard_map/jit(_solve_triangular)/triangular_solve | solution.py:25
  291.0 0.0 copy-done.1
  291.0 0.2 fusion.5
  291.1 0.2 convolution_subtract_fusion.1
  291.3 0.2 fusion.4
  291.5 0.6 fusion.10
  292.2 30.6 %all_gather.7 = bf16[128,256]{1,0:T(8,128)(2,1)S(1)} all-gather(bf16[16,256]{1,0:T(8,128)(2,1)S(1)} %get-tuple-element.18), channel_id=1, replica_groups=mesh['rows'=4,'feat'=8] {'feat'}, dimensions={0}, use_global_device_ids=true | all-gather | bytes 73728 | tf_op jit(solution)/shard_map/all_gather | solution.py:26
  322.7 4.7 fusion.14
  327.4 0.0 all-reduce.9.cloned.1.call-update
  327.4 153.0 %all-reduce.9.cloned.1.call-done = f32[256,8192]{1,0:T(8,128)} async-done(((f32[256,8192]{1,0:T(8,128)}), f32[256,8192]{1,0:T(8,128)}) %all-reduce.9.cloned.1.call-update) | async-done | bytes 8388624 | tf_op jit(solution)/shard_map/psum | solution.py:30
  480.4 7.7 %broadcast_multiply_fusion = f32[256,8192]{1,0:T(8,128)} fusion(f32[256,8192]{1,0:T(8,128)} %all-reduce.9.cloned.1.call-done), kind=kLoop, calls=%fused_computation.5 | loop fusion | flops 2097152 | bytes 16777216 | tf_op jit(solution)/shard_map/div | solution.py:30
  (9 shorter events, 0.1 us)
Async XLA Ops:
  7.2 114.5 %reduce-scatter.2.cloned.1.call-start = ((), (), s32[]{:S(2)}) async-start(), calls=%async_computation.1 | async-start | bytes 147456 | tf_op jit(solution)/shard_map/reduce_scatter | solution.py:16
  39.9 18.2 %copy-start = (bf16[8192,256]{1,0:T(8,128)(2,1)S(1)}, bf16[8192,256]{1,0:T(8,128)(2,1)}, u32[]{:S(2)}) copy-start(bf16[8192,256]{1,0:T(8,128)(2,1)} %param.7) | copy-start | bytes 12582916
  59.6 135.6 %all-reduce.5.cloned.1.call-start = ((), (), s32[]{:S(2)}) async-start(), calls=%async_computation.2 | async-start | bytes 524288 | tf_op jit(solution)/shard_map/psum | solution.py:23
  121.6 169.4 %copy-start.1 = (f32[16,256]{1,0:T(8,128)S(1)}, f32[16,256]{1,0:T(8,128)}, u32[]{:S(2)}) copy-start(f32[16,256]{1,0:T(8,128)} %reduce-scatter.2.cloned.1.call-done) | copy-start | bytes 49156
  123.6 105.3 %all-reduce.7.cloned.1.call-start = ((), (), s32[]{:S(2)}) async-start(), calls=%async_computation.3 | async-start | bytes 524288 | tf_op jit(solution)/shard_map/psum | solution.py:23
  195.2 285.2 %all-reduce.9.cloned.1.call-start = ((), (), s32[]{:S(2)}) async-start(), calls=%async_computation.4 | async-start | bytes 16777216 | tf_op jit(solution)/shard_map/psum | solution.py:30
Sparse Core Ops, SparseCore 0:
  59.7 61.8 reduce-scatter.1
  125.5 69.5 all-reduce.4
  197.6 31.2 all-reduce.6
  327.5 152.7 all-reduce.8
